TPU v7x, 32 devices: a whole 2x2x4 slice. The times are simulated.
32 devices in a mesh: dp: 8 (over y, x, core), tensor: 4 (over z).
Axes of the slice: x: 2, y: 2, z: 4, core: 2. Of those that a mesh axis runs over, the one named last changes fastest.
Arguments:
- hidden_in: bfloat16 [16384, 1024], P('dp'), may hold values from -6 to 6
- lengths: int32 [8], P('dp'), may hold values from 512 to 2048, as said below
- query_weight: bfloat16 [1024, 1024], P(None, 'tensor'), may hold values from -0.1875 to 0.1875
- query_bias: bfloat16 [1024], P('tensor'), may hold values from -1 to 1
- key_weight: bfloat16 [1024, 1024], P(None, 'tensor'), may hold values from -0.1875 to 0.1875
- value_weight: bfloat16 [1024, 1024], P(None, 'tensor'), may hold values from -0.1875 to 0.1875
- value_bias: bfloat16 [1024], P('tensor'), may hold values from -1 to 1
- output_weight: bfloat16 [1024, 1024], P(None, 'tensor'), may hold values from -2 to 2
- output_bias: bfloat16 [1024], replicated, may hold values from -1 to 1
- first_gain: bfloat16 [1024], replicated, may hold values from 0.5 to 1.5
- first_shift: bfloat16 [1024], replicated, may hold values from -1 to 1
- inner_weight: bfloat16 [1024, 4096], P(None, 'tensor'), may hold values from -0.1875 to 0.1875
- inner_bias: bfloat16 [4096], P('tensor'), may hold values from -1 to 1
- outer_weight: bfloat16 [1024, 4096], P(None, 'tensor'), may hold values from -0.125 to 0.125
- outer_bias: bfloat16 [1024], replicated, may hold values from -1 to 1
- second_gain: bfloat16 [1024], replicated, may hold values from 0.5 to 1.5
- second_shift: bfloat16 [1024], replicated, may hold values from -1 to 1
- cotangent: bfloat16 [16384, 1024], P('dp'), may hold values from -6 to 6
- teacher: bfloat16 [16384, 1024], P('dp'), may hold values from -6 to 6
Outputs:
- layer_output: bfloat16 [16384, 1024], P(('dp', 'tensor'))
- distill_loss: float32 [], replicated
- input_grad: float32 [16384, 1024], P(('dp', 'tensor'))
- query_weight_grad: float32 [1024, 1024], P('dp', 'tensor')
- query_bias_grad: float32 [1024], replicated
- key_weight_grad: float32 [1024, 1024], P('dp', 'tensor')
- value_weight_grad: float32 [1024, 1024], P('dp', 'tensor')
- value_bias_grad: float32 [1024], replicated
- output_weight_grad: float32 [1024, 1024], P('dp', 'tensor')
- output_bias_grad: float32 [1024], replicated
- first_gain_grad: float32 [1024], replicated
- first_shift_grad: float32 [1024], replicated
- inner_weight_grad: float32 [1024, 4096], P('dp', 'tensor')
- inner_bias_grad: float32 [4096], replicated
- outer_weight_grad: float32 [1024, 4096], P('dp', 'tensor')
- outer_bias_grad: float32 [1024], replicated
- second_gain_grad: float32 [1024], replicated
- second_shift_grad: float32 [1024], replicated
Inputs may be any that keep to these rules, and one draw needn't show every extreme that they name: `lengths`: one sequence's valid tokens; slots after them are padding; some sequence fills all 2048 slots.
All inputs are finite; a program needn't handle non-finite values.
Results may differ from a plain program's by a relative error of at most 0.018.
Values may be sent and summed in bfloat16 or wider, within the bound.
No kernel may reach another device: no remote copies, remote signals or barrier semaphores. Data moves between devices by JAX's collectives and lax.ppermute only.
A program may use at most 256 MiB of HBM per device.

v0:
```python
import math
import jax
import jax.numpy as jnp
from jax import lax
from jax.sharding import PartitionSpec as P

HD = 64
epsilon = 1e-05


def matmul(former, latter):
    return jnp.dot(former, latter, preferred_element_type=jnp.float32)


def times_rows(former, latter):
    return lax.dot_general(
        former, latter, (((1,), (1,)), ((), ())), preferred_element_type=jnp.float32
    )


def over_rows(former, latter):
    return lax.dot_general(
        former, latter, (((0,), (0,)), ((), ())), preferred_element_type=jnp.float32
    )


def layer_norm(hidden, norm_gain, norm_shift):
    centered = hidden - jnp.mean(hidden, axis=-1, keepdims=True)
    inverse = lax.rsqrt(jnp.mean(centered * centered, axis=-1, keepdims=True) + epsilon)
    normal = centered * inverse
    return (normal * norm_gain + norm_shift, normal, inverse)


def norm_back(upstream, normal, inverse, norm_gain):
    scaled = upstream * norm_gain
    return inverse * (
        scaled
        - jnp.mean(scaled, axis=-1, keepdims=True)
        - normal * jnp.mean(scaled * normal, axis=-1, keepdims=True)
    )


def gelu_exact(values):
    return 0.5 * values * (1.0 + jax.scipy.special.erf(values * 0.7071067811865476))


def gelu_slope(values):
    return (
        0.5 * (1.0 + jax.scipy.special.erf(values * 0.7071067811865476))
        + values * jnp.exp(-0.5 * values * values) * 0.3989422804014327
    )


def split_blocks(queries, keys_all, values_all):
    seq_len, local_width = queries.shape
    heads_here = local_width // HD
    block_rows = min(512, seq_len)
    block_count = seq_len // block_rows
    keys_split = keys_all.reshape(seq_len, heads_here, HD)
    values_split = values_all.reshape(seq_len, heads_here, HD)
    query_blocks = queries.reshape(block_count, block_rows, heads_here, HD)
    return (keys_split, values_split, query_blocks, block_count, block_rows, heads_here)


def block_scores(query_block, keys_split, key_valid, score_scale):
    scores = (
        jnp.einsum("qhd,khd->hqk", query_block, keys_split, preferred_element_type=jnp.float32)
        * score_scale
    )
    return jnp.where(key_valid[None, None, :], scores, -1e30)


def attend_forward(queries, keys_all, values_all, key_valid, score_scale):
    keys_split, values_split, query_blocks, block_count, block_rows, heads_here = split_blocks(
        queries, keys_all, values_all
    )

    def one_block(query_block):
        scores = block_scores(query_block, keys_split, key_valid, score_scale)
        row_peak = jnp.max(scores, axis=-1, keepdims=True)
        exponent = jnp.exp(scores - row_peak)
        row_total = jnp.sum(exponent, axis=-1, keepdims=True)
        probs = (exponent / row_total).astype(jnp.bfloat16)
        context = jnp.einsum(
            "hqk,khd->qhd", probs, values_split, preferred_element_type=jnp.float32
        )
        return (context, (row_peak + jnp.log(row_total))[..., 0])

    context, logsum = lax.map(one_block, query_blocks)
    return (context.reshape(queries.shape), logsum)


def attend_backward(queries, keys_all, values_all, key_valid, score_scale, logsum, context_grad):
    keys_split, values_split, query_blocks, block_count, block_rows, heads_here = split_blocks(
        queries, keys_all, values_all
    )
    grad_blocks = context_grad.reshape(block_count, block_rows, heads_here, HD)

    def one_block(carry, inputs):
        key_sum, value_sum = carry
        query_block, grad_block, logsum_block = inputs
        scores = block_scores(query_block, keys_split, key_valid, score_scale)
        probs = jnp.exp(scores - logsum_block[..., None])
        prob_grad = jnp.einsum(
            "qhd,khd->hqk", grad_block, values_split, preferred_element_type=jnp.float32
        )
        centre = jnp.sum(probs * prob_grad, axis=-1, keepdims=True)
        score_grad = (probs * (prob_grad - centre)).astype(jnp.bfloat16)
        query_grad = (
            jnp.einsum("hqk,khd->qhd", score_grad, keys_split, preferred_element_type=jnp.float32)
            * score_scale
        )
        key_sum = (
            key_sum
            + jnp.einsum(
                "hqk,qhd->khd", score_grad, query_block, preferred_element_type=jnp.float32
            )
            * score_scale
        )
        value_sum = value_sum + jnp.einsum(
            "hqk,qhd->khd",
            probs.astype(jnp.bfloat16),
            grad_block,
            preferred_element_type=jnp.float32,
        )
        return ((key_sum, value_sum), query_grad)

    zero_block = jnp.zeros(keys_split.shape, jnp.float32)
    (key_sum, value_sum), query_grads = lax.scan(
        one_block, (zero_block, zero_block), (query_blocks, grad_blocks, logsum)
    )
    return (
        query_grads.reshape(queries.shape),
        key_sum.reshape(queries.shape),
        value_sum.reshape(queries.shape),
    )


def shards(
    hidden_in,
    lengths,
    query_weight,
    query_bias,
    key_weight,
    value_weight,
    value_bias,
    output_weight,
    output_bias,
    first_gain,
    first_shift,
    inner_weight,
    inner_bias,
    outer_weight,
    outer_bias,
    second_gain,
    second_shift,
    cotangent,
    teacher,
):
    seq_len, model_width = hidden_in.shape
    tensor_size = lax.axis_size("tensor")
    tensor_index = lax.axis_index("tensor")
    share_rows = seq_len // tensor_size
    row_start = tensor_index * share_rows
    score_scale = 1.0 / math.sqrt(HD)
    positions = jnp.arange(seq_len, dtype=jnp.int32)
    row_valid = positions < lengths[0]
    token_total = lax.psum(jnp.sum(lengths), "dp").astype(jnp.float32)
    grad_scale = seq_len * lax.axis_size("dp") / (2.0 * token_total)
    hidden_float = hidden_in.astype(jnp.float32)
    queries = (matmul(hidden_in, query_weight) + query_bias).astype(jnp.bfloat16)
    keys_all = matmul(hidden_in, key_weight).astype(jnp.bfloat16)
    values_all = (matmul(hidden_in, value_weight) + value_bias).astype(jnp.bfloat16)
    context, logsum = attend_forward(queries, keys_all, values_all, row_valid, score_scale)
    context_low = context.astype(jnp.bfloat16)
    attention_part = times_rows(context_low, output_weight)

    def take_own(array_in):
        return lax.dynamic_slice_in_dim(array_in, row_start, share_rows, 0)

    attention_whole = lax.psum(attention_part, "tensor")
    normed, normal_one, inverse_one = layer_norm(
        hidden_float + (attention_whole + output_bias), first_gain, first_shift
    )
    normed_low = normed.astype(jnp.bfloat16)
    inner = matmul(normed_low, inner_weight) + inner_bias
    activated = gelu_exact(inner).astype(jnp.bfloat16)
    outer_part = times_rows(activated, outer_weight)
    outer_rows = lax.psum(outer_part, "tensor")
    final, normal_two, inverse_two = layer_norm(
        normed + (outer_rows + outer_bias), second_gain, second_shift
    )
    row_mask = row_valid[:, None]
    difference = final - teacher.astype(jnp.float32)
    loss_part = jnp.sum(take_own(jnp.where(row_mask, difference * difference, 0.0)))
    final_grad = jnp.where(row_mask, cotangent.astype(jnp.float32) + grad_scale * difference, 0.0)
    second_grad = norm_back(final_grad, normal_two, inverse_two, second_gain)
    branch_low = second_grad.astype(jnp.bfloat16)
    activated_grad = matmul(branch_low, outer_weight)
    outer_weight_grad = over_rows(branch_low, activated)
    inner_low = (activated_grad * gelu_slope(inner)).astype(jnp.bfloat16)
    inner_bias_grad = jnp.sum(inner_low.astype(jnp.float32), axis=0)
    inner_weight_grad = over_rows(normed_low, inner_low)
    normed_part = times_rows(inner_low, inner_weight)
    normed_back = lax.psum(normed_part, "tensor")
    normed_grad = second_grad + normed_back
    first_grad = norm_back(normed_grad, normal_one, inverse_one, first_gain)
    attention_low = first_grad.astype(jnp.bfloat16)
    output_weight_grad = over_rows(attention_low, context_low)
    context_grad = matmul(attention_low, output_weight).astype(jnp.bfloat16)
    query_grad, key_grad, value_grad = attend_backward(
        queries, keys_all, values_all, row_valid, score_scale, logsum, context_grad
    )
    query_low = query_grad.astype(jnp.bfloat16)
    key_low = key_grad.astype(jnp.bfloat16)
    value_low = value_grad.astype(jnp.bfloat16)
    input_part = (
        times_rows(query_low, query_weight)
        + times_rows(key_low, key_weight)
        + times_rows(value_low, value_weight)
    )
    input_back = lax.psum(input_part.astype(jnp.bfloat16), "tensor").astype(jnp.float32)
    input_rows = take_own(input_back) + take_own(first_grad)
    weight_grads = (
        lax.psum_scatter(
            over_rows(hidden_in, query_low).astype(jnp.bfloat16),
            "dp",
            scatter_dimension=0,
            tiled=True,
        ).astype(jnp.float32),
        lax.psum_scatter(
            over_rows(hidden_in, key_low).astype(jnp.bfloat16),
            "dp",
            scatter_dimension=0,
            tiled=True,
        ).astype(jnp.float32),
        lax.psum_scatter(
            over_rows(hidden_in, value_low).astype(jnp.bfloat16),
            "dp",
            scatter_dimension=0,
            tiled=True,
        ).astype(jnp.float32),
        lax.psum_scatter(
            output_weight_grad.astype(jnp.bfloat16), "dp", scatter_dimension=0, tiled=True
        ).astype(jnp.float32),
        lax.psum_scatter(
            inner_weight_grad.astype(jnp.bfloat16), "dp", scatter_dimension=0, tiled=True
        ).astype(jnp.float32),
        lax.psum_scatter(
            outer_weight_grad.astype(jnp.bfloat16), "dp", scatter_dimension=0, tiled=True
        ).astype(jnp.float32),
    )

    def placed(vector_in):
        full_zeros = jnp.zeros((vector_in.shape[0] * tensor_size,), jnp.float32)
        return lax.dynamic_update_slice_in_dim(
            full_zeros, vector_in, tensor_index * vector_in.shape[0], 0
        )

    vector_grads = lax.psum(
        (
            placed(jnp.sum(query_low.astype(jnp.float32), axis=0)),
            placed(jnp.sum(value_low.astype(jnp.float32), axis=0)),
            jnp.sum(take_own(attention_low).astype(jnp.float32), axis=0),
            jnp.sum(take_own(normed_grad * normal_one), axis=0),
            jnp.sum(take_own(normed_grad), axis=0),
            placed(inner_bias_grad),
            jnp.sum(take_own(branch_low).astype(jnp.float32), axis=0),
            jnp.sum(take_own(final_grad * normal_two), axis=0),
            jnp.sum(take_own(final_grad), axis=0),
            loss_part,
        ),
        ("dp", "tensor"),
    )
    (
        query_bias_grad,
        value_bias_grad,
        output_bias_grad,
        first_gain_grad,
        first_shift_grad,
        inner_bias_full,
        outer_bias_grad,
        second_gain_grad,
        second_shift_grad,
        loss_total,
    ) = vector_grads
    (
        query_weight_grad,
        key_weight_grad,
        value_weight_grad,
        output_weight_sum,
        inner_weight_sum,
        outer_weight_sum,
    ) = weight_grads
    distill_loss = loss_total / token_total
    return (
        take_own(final).astype(jnp.bfloat16),
        distill_loss,
        input_rows,
        query_weight_grad,
        query_bias_grad,
        key_weight_grad,
        value_weight_grad,
        value_bias_grad,
        output_weight_sum,
        output_bias_grad,
        first_gain_grad,
        first_shift_grad,
        inner_weight_sum,
        inner_bias_full,
        outer_weight_sum,
        outer_bias_grad,
        second_gain_grad,
        second_shift_grad,
    )


def solution(mesh):
    in_specs = (
        P("dp", None),
        P("dp"),
        P(None, "tensor"),
        P("tensor"),
        P(None, "tensor"),
        P(None, "tensor"),
        P("tensor"),
        P(None, "tensor"),
        P(),
        P(),
        P(),
        P(None, "tensor"),
        P("tensor"),
        P(None, "tensor"),
        P(),
        P(),
        P(),
        P("dp", None),
        P("dp", None),
    )
    out_specs = (
        P(("dp", "tensor"), None),
        P(),
        P(("dp", "tensor"), None),
        P("dp", "tensor"),
        P(),
        P("dp", "tensor"),
        P("dp", "tensor"),
        P(),
        P("dp", "tensor"),
        P(),
        P(),
        P(),
        P("dp", "tensor"),
        P(),
        P("dp", "tensor"),
        P(),
        P(),
        P(),
    )
    return jax.shard_map(shards, mesh=mesh, in_specs=in_specs, out_specs=out_specs, check_vma=False)
```

profile of v0, /device:TPU:0, one launch (start us, length us, event | category | flops | bytes accessed | tf_op | source)
XLA Modules:
  0.0 1564.1 jit_solution(17279428161375169190)
XLA Ops:
  8.7 3.6 fusion.52
  14.1 4.0 copy.54
  18.1 3.7 convolution_convert_fusion.1
  25.2 55.2 %while.28 = (s32[]{:T(128)}, bf16[4,512,4,64]{1,3,2,0:T(8,128)(2,1)}, f32[4,4,512]{2,1,0:T(4,128)S(1)}, bf16[4,512,4,64]{1,3,2,0:T(8,128)(2,1)}, bf16[2048,4,64]...) while((s32[]{:T(128)}, bf16[4,512,4,64]{1,3,2,0:T(8,128)(2,1)}, ...), condition=%wide.region_3.4_spmd.clone, body=%wide.region_0.3_spmd.clone.sunk | while | flops 1124073472 | bytes 65872064 | solution.py:89
  25.9 3.5 fusion.136
  29.4 3.7 fusion.137
  33.2 4.9 fusion.138
  43.2 3.7 fusion.137
  47.0 4.9 fusion.138
  53.5 3.5 fusion.136
  57.0 3.7 fusion.137
  60.8 4.9 fusion.138
  70.8 3.7 fusion.137
  74.6 4.9 fusion.138
  83.8 5.6 fusion.70
  89.8 293.4 %all-reduce.6.cloned.1.call-done = f32[2048,1024]{1,0:T(8,128)} async-done(((f32[2048,1024]{1,0:T(8,128)}), f32[2048,1024]{1,0:T(8,128)}) %all-reduce.6.cloned.1.call-update) | async-done | bytes 8388624 | tf_op jit(solution)/shard_map/psum | solution.py:181
  383.2 5.9 fusion.54
  394.8 7.4 multiply_convert_fusion.1
  404.1 6.9 fusion.71
  411.0 8.8 psum.108
  421.3 279.7 %all-reduce.8.cloned.1.call-done = f32[2048,1024]{1,0:T(8,128)} async-done(((f32[2048,1024]{1,0:T(8,128)}), f32[2048,1024]{1,0:T(8,128)}) %all-reduce.8.cloned.1.call-update) | async-done | bytes 8388624 | tf_op jit(solution)/shard_map/psum | solution.py:189
  701.0 6.7 fusion.69
  708.8 10.9 multiply_reduce_fusion.6
  725.8 11.3 convert_reduce_fusion
  739.1 6.9 fusion.72
  746.5 9.4 convolution_convert_fusion.2
  756.0 10.5 convolution_convert_fusion.3
  766.7 269.2 %all-reduce.10.cloned.1.call-done = f32[2048,1024]{1,0:T(8,128)} async-done(((f32[2048,1024]{1,0:T(8,128)}), f32[2048,1024]{1,0:T(8,128)}) %all-reduce.10.cloned.1.call-update) | async-done | bytes 8388624 | tf_op jit(solution)/shard_map/psum | solution.py:205
  1036.0 16.3 %multiply_reduce_fusion.5 = (f32[2048]{0:T(1024)S(1)}, f32[2048]{0:T(1024)S(1)}, f32[2048,1024]{1,0:T(8,128)}) fusion(f32[1024]{0:T(1024)S(1)} %convert_element_type.183, f32[2048,1024]{1,0:T(8,128)} %copy-done.5, f32[2048,1024]{1,0:T(8,128)} %all-reduce.10.cloned.1.call-done, f32[2048,1024]{1,0:T(8,128)} %copy-done.7, f32[2048]{0:T(1024)S(1)} %get-tuple-element.345, ...), kind=kLoop, calls=%fused_computation.76 | loop fusion | flops 20967424 | bytes 41992192 | tf_op jit(solution)/shard_map/reduce_sum | solution.py:38
  1052.4 9.8 fusion.67
  1066.3 4.4 reshape.147
  1070.8 4.1 copy.58
  1076.0 166.5 %while.29 = (s32[]{:T(128)}, f32[2048,4,64]{0,2,1:T(8,128)S(1)}, f32[2048,4,64]{0,2,1:T(8,128)}, bf16[4,512,4,64]{1,3,2,0:T(8,128)(2,1)}, bf16[4,512,4,64]{1,3,2...) while((s32[]{:T(128)}, f32[2048,4,64]{0,2,1:T(8,128)S(1)}, ...), condition=%wide.region_20.21_spmd.clone, body=%wide.region_18.20_spmd.clone.sunk | while | flops 2750021632 | bytes 180945136 | solution.py:129
  1077.2 3.7 fusion.148
  1080.9 5.8 fusion.150
  1086.7 10.1 multiply_reduce_fusion.8
  1096.8 11.0 multiply_convert_fusion.3
  1107.8 7.2 fusion.151
  1118.9 3.7 fusion.148
  1122.6 6.2 fusion.150
  1128.8 9.9 multiply_reduce_fusion.8
  1138.7 10.6 multiply_convert_fusion.3
  1149.3 7.1 fusion.151
  1160.3 3.7 fusion.148
  1164.0 6.2 fusion.150
  1170.2 9.9 multiply_reduce_fusion.8
  1180.1 10.6 multiply_convert_fusion.3
  1190.7 7.1 fusion.151
  1201.8 3.7 fusion.148
  1205.5 6.2 fusion.150
  1211.7 9.9 multiply_reduce_fusion.8
  1221.6 10.6 multiply_convert_fusion.3
  1232.2 7.1 fusion.151
  1257.7 3.5 fusion.61
  1262.3 5.7 fusion.74
  1268.0 4.4 convolution_convert_fusion.4
  1272.5 4.5 fusion.73
  1277.1 9.1 add_convert_fusion
  1291.3 4.6 dynamic-slice_reduce_fusion
  1304.3 40.3 %all-reduce = (f32[]{:T(128)}, f32[1024]{0:T(1024)}, f32[1024]{0:T(1024)}, f32[1024]{0:T(1024)}, f32[1024]{0:T(1024)}, /*index=5*/f32[1024]{0:T(1024)}, f32[4096...) all-reduce(f32[]{:T(128)} %get-tuple-element.344, ...), channel_id=1, replica_groups=mesh['dp'=8,'tensor'=4] {'dp','tensor'}, use_global_device_ids=true, to_apply=%region_11.12 | all-reduce | flops 12289 | bytes 98312 | tf_op jit(solution)/shard_map/psum | solution.py:260
  1348.7 8.8 reduce-scatter.23.cloned.1.call-done
  1359.3 35.5 %reduce-scatter.13.cloned.1.call-done = bf16[128,256]{1,0:T(8,128)(2,1)} async-done(((bf16[1024,256]{1,0:T(8,128)(2,1)}), bf16[128,256]{1,0:T(8,128)(2,1)}) %reduce-scatter.13.cloned.1.call-update) | async-done | bytes 65552 | tf_op jit(solution)/shard_map/reduce_scatter | solution.py:243
  1396.3 155.7 %all-reduce.12.cloned.1.call-done = bf16[2048,1024]{1,0:T(8,128)(2,1)} async-done(((bf16[2048,1024]{1,0:T(8,128)(2,1)}), bf16[2048,1024]{1,0:T(8,128)(2,1)}) %all-reduce.12.cloned.1.call-update) | async-done | bytes 4194320 | tf_op jit(solution)/shard_map/psum | solution.py:222
  1552.0 3.6 dynamic-slice_add_fusion
  (225 shorter events, 98.7 us)
Async XLA Ops:
  7.2 387.5 %copy-start = (bf16[1024,1024]{1,0:T(8,128)(2,1)S(1)}, bf16[1024,1024]{1,0:T(8,128)(2,1)}, u32[]{:S(2)}) copy-start(bf16[1024,1024]{1,0:T(8,128)(2,1)} %param.34) | copy-start | bytes 6291460
  7.2 376.0 %all-reduce.6.cloned.1.call-start = ((), (), s32[]{:S(2)}) async-start(), calls=%async_computation.6 | async-start | bytes 16777216 | tf_op jit(solution)/shard_map/psum | solution.py:181
  18.1 3.8 copy-start.9
  18.1 3.8 copy-start.25
  29.4 3.8 copy-start.11
  29.4 3.8 copy-start.21
  43.2 3.8 copy-start.11
  43.2 3.8 copy-start.21
  57.0 3.8 copy-start.11
  57.0 3.8 copy-start.21
  65.7 1.0 copy-start.22
  70.8 3.8 copy-start.11
  70.8 3.8 copy-start.21
  82.8 1.1 copy-start.15
  83.8 5.9 copy-start.29
  83.8 5.9 copy-start.30
  83.8 6.0 copy-start.31
  83.8 6.0 copy-start.32
  89.5 611.5 %all-reduce.8.cloned.1.call-start = ((), (), s32[]{:S(2)}) async-start(), calls=%async_computation.7 | async-start | bytes 16777216 | tf_op jit(solution)/shard_map/psum | solution.py:189
  383.2 7.0 copy-start.8
  383.2 8.2 copy-start.10
  394.7 7.4 copy-start.5
  394.8 9.3 copy-start.36
  402.1 1.9 copy-start.38
  411.0 10.2 copy-start.33
  411.0 10.2 copy-start.34
  411.0 10.2 copy-start.35
  411.0 625.0 %all-reduce.10.cloned.1.call-start = ((), (), s32[]{:S(2)}) async-start(), calls=%async_computation.8 | async-start | bytes 16777216 | tf_op jit(solution)/shard_map/psum | solution.py:205
  421.3 287.5 %copy-start.27 = (pred[2048]{0:T(1024)(128)(4,1)}, pred[2048]{0:T(1024)(128)(4,1)S(1)}, u32[]{:S(2)}) copy-start(pred[2048]{0:T(1024)(128)(4,1)S(1)} %iota_compare_fusion.2) | copy-start | bytes 6148
  719.7 3.5 copy-start.6
  719.7 6.1 copy-start.7
  719.7 6.1 copy-start.37
  725.8 11.3 copy-start.13
  737.1 2.0 copy-start.39
  746.0 549.9 %reduce-scatter.17.cloned.1.call-start = ((), (), s32[]{:S(2)}) async-start(), calls=%async_computation.12 | async-start | bytes 2359296 | tf_op jit(solution)/shard_map/reduce_scatter | solution.py:249
  756.0 541.7 %reduce-scatter.15.cloned.1.call-start = ((), (), s32[]{:S(2)}) async-start(), calls=%async_computation.11 | async-start | bytes 2359296 | tf_op jit(solution)/shard_map/reduce_scatter | solution.py:246
  766.5 578.7 %reduce-scatter.19.cloned.1.call-start = ((), (), s32[]{:S(2)}) async-start(), calls=%async_computation.13 | async-start | bytes 589824
  1052.3 11.8 copy-start.23
  1062.1 2.0 copy-start.14
  1076.2 1.0 copy-start.3
  1107.8 7.2 copy-start.2
  1115.0 2.9 copy-start.4
  1117.9 1.0 copy-start.3
  1149.3 7.1 copy-start.2
  1156.5 2.9 copy-start.4
  1159.3 1.0 copy-start.3
  1190.7 7.2 copy-start.2
  1197.9 2.9 copy-start.4
  1200.8 1.0 copy-start.3
  1232.2 7.2 copy-start.2
  1239.3 2.9 copy-start.4
  1244.8 1.0 copy-start.17
  1250.3 96.8 %reduce-scatter.21.cloned.1.call-start = ((), (), s32[]{:S(2)}) async-start(), calls=%async_computation.14 | async-start | bytes 589824
  1256.8 100.8 %reduce-scatter.23.cloned.1.call-start = ((), (), s32[]{:S(2)}) async-start(), calls=%async_computation.15 | async-start | bytes 589824
  1261.2 6.8 copy-start.16
  1262.3 10.2 copy-start.18
  1267.9 4.5 copy-start.24
  1267.9 126.8 %reduce-scatter.13.cloned.1.call-start = ((), (), s32[]{:S(2)}) async-start(), calls=%async_computation.10 | async-start | bytes 589824 | tf_op jit(solution)/shard_map/reduce_scatter | solution.py:243
  1272.5 4.6 copy-start.20
  1272.5 4.6 copy-start.26
  1277.0 10.1 copy-start.28
  1277.0 275.0 %all-reduce.12.cloned.1.call-start = ((), (), s32[]{:S(2)}) async-start(), calls=%async_computation.9 | async-start | bytes 8388608 | tf_op jit(solution)/shard_map/psum | solution.py:222
  1286.2 13.3 copy-start.12
  1291.3 264.3 %copy-start.1 = (bf16[1024,1024]{1,0:T(8,128)(2,1)S(1)}, bf16[1024,1024]{1,0:T(8,128)(2,1)}, u32[]{:S(2)}) copy-start(bf16[1024,1024]{1,0:T(8,128)(2,1)} %param.34) | copy-start | bytes 6291460
  (4 other events, 3.9 us)
Sparse Core Ops, SparseCore 0:
  89.6 293.5 all-reduce.5
  411.1 289.7 all-reduce.7
  746.1 289.8 all-reduce.9
  1039.1 40.0 reduce-scatter.16
  1082.4 41.1 reduce-scatter.14
  1250.4 32.5 reduce-scatter.18
  1286.1 34.2 reduce-scatter.20
  1323.4 34.0 reduce-scatter.22
  1360.6 34.0 reduce-scatter.12
  1397.0 154.9 all-reduce.11
where the time goes:
time: 1570 us; the launch traced here: 1560 us
  waiting for transfers between devices  1040 us (66%)
  matrix products  256 us (16%)
  other arithmetic  142 us (9%)
  local copies, waits for them, and re-layouts  53.8 us (3%)
  blocking collectives  49.1 us (3%)
  between operations  18.3 us (1%)
    psum x1, waiting for transfers between devices, shards(): attention_whole = lax.psum(attention_part, 'tensor')  293 us
    psum x1, waiting for transfers between devices, shards(): outer_rows = lax.psum(outer_part, 'tensor')  280 us
    psum x1, waiting for transfers between devices, shards(): normed_back = lax.psum(normed_part, 'tensor')  269 us
    psum x1, waiting for transfers between devices, shards(): lax.psum(input_part.astype(jnp.bfloat16), 'tensor').astype(jnp.float32)  156 us
    convert_element_type x4, other arithmetic, one_block(): score_grad = (probs * (prob_grad - centre)).astype(jnp.bfloat16)  42.8 us
    psum x1, blocking collectives, shards(): lax.psum((placed(jnp.sum(query_low.astype(jnp.float32), axis=0)), placed(...  40.3 us
    dot_general x4, matrix products, one_block(): jnp.einsum('qhd,khd->hqk', grad_block, values_split, preferred_element_ty...  39.8 us
    dot_general x6, matrix products, times_rows(): lax.dot_general(former, latter, (((1,), (1,)), ((), ())), preferred_eleme...  38.7 us
  transfers between devices with their start and end apart: 10, of which 6 were waited for; matrix products, arithmetic and copies ran while one was open for 18% of the time, Pallas kernels for 0%

commit v1 on v0

--- a/solution.py
+++ b/solution.py
@@ -1,3 +1,4 @@
+import functools
 import math
 import jax
 import jax.numpy as jnp
@@ -6,6 +7,21 @@
 
 HD = 64
 epsilon = 1e-05
+
+
+def search_bands_on_mesh(panel, peer_axis):
+    n_lanes = lax.axis_size(peer_axis)
+
+    def prepare_the_boxes(extra, lower):
+        if lower >= n_lanes:
+            return extra
+        field_out = tuple(((k0, k0 ^ lower) for k0 in range(n_lanes)))
+        return prepare_the_boxes(extra + lax.ppermute(extra, peer_axis, field_out), 2 * lower)
+
+    return prepare_the_boxes(panel, 1)
+
+
+write_spot = functools.partial(search_bands_on_mesh, peer_axis="tensor")
 
 
 def matmul(former, latter):
@@ -186,7 +202,7 @@
     inner = matmul(normed_low, inner_weight) + inner_bias
     activated = gelu_exact(inner).astype(jnp.bfloat16)
     outer_part = times_rows(activated, outer_weight)
-    outer_rows = lax.psum(outer_part, "tensor")
+    outer_rows = write_spot(outer_part)
     final, normal_two, inverse_two = layer_norm(
         normed + (outer_rows + outer_bias), second_gain, second_shift
     )

time: 1570 us -> 1840 us (1.17)
  waiting for transfers between devices: 1040 us -> 1290 us
    ppermute x0 -> x2, waiting for transfers between devices: none -> 529 us  [prepare_the_boxes(): lax.ppermute(extra, peer_axis, field_out)]
    psum x1 -> x0, waiting for transfers between devices: 280 us -> none  [shards(): outer_rows = lax.psum(outer_part, 'tensor')]
  transfers between devices with their start and end apart: 10 -> 11, of which waited for: 6 -> 7; matrix products, arithmetic and copies ran while one was open for 18% -> 16% of each run, Pallas kernels for 0% -> 0%
where the time goes in v1:
time: 1840 us; the launch traced here: 1830 us
  waiting for transfers between devices  1290 us (70%)
  matrix products  254 us (14%)
  other arithmetic  156 us (8%)
  local copies, waits for them, and re-layouts  55 us (3%)
  blocking collectives  49.4 us (3%)
    ppermute x2, waiting for transfers between devices, prepare_the_boxes(): lax.ppermute(extra, peer_axis, field_out)  529 us
    psum x1, waiting for transfers between devices, shards(): attention_whole = lax.psum(attention_part, 'tensor')  293 us
    psum x1, waiting for transfers between devices, shards(): normed_back = lax.psum(normed_part, 'tensor')  270 us
    psum x1, waiting for transfers between devices, shards(): lax.psum(input_part.astype(jnp.bfloat16), 'tensor').astype(jnp.float32)  156 us
    convert_element_type x4, other arithmetic, one_block(): score_grad = (probs * (prob_grad - centre)).astype(jnp.bfloat16)  42.8 us
    psum x1, blocking collectives, shards(): lax.psum((placed(jnp.sum(query_low.astype(jnp.float32), axis=0)), placed(...  40.3 us
    dot_general x4, matrix products, one_block(): jnp.einsum('qhd,khd->hqk', grad_block, values_split, preferred_element_ty...  39.8 us
  transfers between devices with their start and end apart: 11, of which 7 were waited for; matrix products, arithmetic and copies ran while one was open for 16% of the time, Pallas kernels for 0%

profile of v1, /device:TPU:0, one launch (start us, length us, event | category | flops | bytes accessed | tf_op | source)
XLA Modules:
  0.0 1829.2 jit_solution(17261489836693598658)
XLA Ops:
  8.7 3.6 fusion.52
  14.1 4.0 copy.54
  18.1 3.7 convolution_convert_fusion.1
  25.2 55.2 %while.28 = (s32[]{:T(128)}, bf16[4,512,4,64]{1,3,2,0:T(8,128)(2,1)}, f32[4,4,512]{2,1,0:T(4,128)S(1)}, bf16[4,512,4,64]{1,3,2,0:T(8,128)(2,1)}, bf16[2048,4,64]...) while((s32[]{:T(128)}, bf16[4,512,4,64]{1,3,2,0:T(8,128)(2,1)}, ...), condition=%wide.region_3.4_spmd.clone, body=%wide.region_0.3_spmd.clone.sunk | while | flops 1124073472 | bytes 65872064 | solution.py:105
  29.4 3.7 fusion.137
  33.2 4.9 fusion.138
  43.2 3.7 fusion.137
  47.0 4.9 fusion.138
  57.0 3.7 fusion.137
  60.8 4.9 fusion.138
  70.8 3.7 fusion.137
  74.6 4.9 fusion.138
  83.9 5.6 fusion.70
  89.9 293.3 %all-reduce.5.cloned.1.call-done = f32[2048,1024]{1,0:T(8,128)} async-done(((f32[2048,1024]{1,0:T(8,128)}), f32[2048,1024]{1,0:T(8,128)}) %all-reduce.5.cloned.1.call-update) | async-done | bytes 8388624 | tf_op jit(solution)/shard_map/psum | solution.py:197
  383.2 5.9 fusion.54
  394.8 7.4 multiply_convert_fusion.1
  402.2 4.6 fusion.71
  410.0 179.0 %collective-permute-done = f32[2048,1024]{1,0:T(8,128)} collective-permute-done((f32[2048,1024]{1,0:T(8,128)S(1)}, f32[2048,1024]{1,0:T(8,128)}, u32[]{:S(2)}, u32[]{:S(2)}) %collective-permute-start) | collective-permute-done | bytes 8388640 | tf_op jit(solution)/shard_map/ppermute | solution.py:19
  589.0 12.0 add.205
  602.4 9.1 psum.100
  612.9 350.2 %collective-permute-done.1 = f32[2048,1024]{1,0:T(8,128)} collective-permute-done((f32[2048,1024]{1,0:T(8,128)}, f32[2048,1024]{1,0:T(8,128)}, u32[]{:S(2)}, u32[]{:S(2)}) %collective-permute-start.1) | collective-permute-done | bytes 8388640 | tf_op jit(solution)/shard_map/ppermute | solution.py:19
  963.2 9.2 fusion.69
  973.6 10.9 multiply_reduce_fusion.6
  990.6 11.3 convert_reduce_fusion
  1003.9 6.9 fusion.72
  1011.0 9.4 convolution_convert_fusion.2
  1020.5 10.5 convolution_convert_fusion.3
  1031.3 270.0 %all-reduce.7.cloned.1.call-done = f32[2048,1024]{1,0:T(8,128)} async-done(((f32[2048,1024]{1,0:T(8,128)}), f32[2048,1024]{1,0:T(8,128)}) %all-reduce.7.cloned.1.call-update) | async-done | bytes 8388624 | tf_op jit(solution)/shard_map/psum | solution.py:221
  1301.3 16.3 multiply_reduce_fusion.5
  1317.7 9.8 fusion.67
  1331.7 4.4 reshape.147
  1336.1 4.1 copy.58
  1341.4 166.7 %while.29 = (s32[]{:T(128)}, f32[2048,4,64]{0,2,1:T(8,128)S(1)}, f32[2048,4,64]{0,2,1:T(8,128)}, bf16[4,512,4,64]{1,3,2,0:T(8,128)(2,1)}, bf16[4,512,4,64]{1,3,2...) while((s32[]{:T(128)}, f32[2048,4,64]{0,2,1:T(8,128)S(1)}, ...), condition=%wide.region_19.20_spmd.clone, body=%wide.region_17.19_spmd.clone.sunk | while | flops 2750021632 | bytes 180945136 | solution.py:145
  1342.7 3.7 fusion.148
  1346.3 5.8 fusion.150
  1352.1 10.1 multiply_reduce_fusion.8
  1362.2 11.0 multiply_convert_fusion.3
  1373.2 7.2 fusion.151
  1384.3 3.7 fusion.148
  1388.0 6.2 fusion.150
  1394.2 9.9 multiply_reduce_fusion.8
  1404.1 10.6 multiply_convert_fusion.3
  1414.7 7.1 fusion.151
  1425.8 3.7 fusion.148
  1429.4 6.2 fusion.150
  1435.6 9.9 multiply_reduce_fusion.8
  1445.5 10.6 multiply_convert_fusion.3
  1456.2 7.1 fusion.151
  1467.2 3.7 fusion.148
  1470.9 6.2 fusion.150
  1477.1 9.9 multiply_reduce_fusion.8
  1487.0 10.6 multiply_convert_fusion.3
  1497.6 7.1 fusion.151
  1523.3 3.5 fusion.61
  1527.9 5.7 fusion.74
  1533.6 4.5 convolution_convert_fusion.4
  1538.1 4.5 fusion.73
  1542.7 9.1 add_convert_fusion
  1556.8 4.6 dynamic-slice_reduce_fusion
  1569.8 40.3 %all-reduce = (f32[]{:T(128)}, f32[1024]{0:T(1024)}, f32[1024]{0:T(1024)}, f32[1024]{0:T(1024)}, f32[1024]{0:T(1024)}, /*index=5*/f32[1024]{0:T(1024)}, f32[4096...) all-reduce(f32[]{:T(128)} %get-tuple-element.344, ...), channel_id=1, replica_groups=mesh['dp'=8,'tensor'=4] {'dp','tensor'}, use_global_device_ids=true, to_apply=%region_10.11 | all-reduce | flops 12289 | bytes 98312 | tf_op jit(solution)/shard_map/psum | solution.py:276
  1614.3 8.8 reduce-scatter.23.cloned.1.call-done
  1624.8 35.5 %reduce-scatter.13.cloned.1.call-done = bf16[128,256]{1,0:T(8,128)(2,1)} async-done(((bf16[1024,256]{1,0:T(8,128)(2,1)}), bf16[128,256]{1,0:T(8,128)(2,1)}) %reduce-scatter.13.cloned.1.call-update) | async-done | bytes 65552 | tf_op jit(solution)/shard_map/reduce_scatter | solution.py:259
  1661.8 155.9 %all-reduce.9.cloned.1.call-done = bf16[2048,1024]{1,0:T(8,128)(2,1)} async-done(((bf16[2048,1024]{1,0:T(8,128)(2,1)}), bf16[2048,1024]{1,0:T(8,128)(2,1)}) %all-reduce.9.cloned.1.call-update) | async-done | bytes 4194320 | tf_op jit(solution)/shard_map/psum | solution.py:238
  1817.7 3.6 dynamic-slice_add_fusion
  (229 shorter events, 108.0 us)
Async XLA Ops:
  7.2 387.6 %copy-start = (bf16[1024,1024]{1,0:T(8,128)(2,1)S(1)}, bf16[1024,1024]{1,0:T(8,128)(2,1)}, u32[]{:S(2)}) copy-start(bf16[1024,1024]{1,0:T(8,128)(2,1)} %param.34) | copy-start | bytes 6291460
  7.2 376.0 %all-reduce.5.cloned.1.call-start = ((), (), s32[]{:S(2)}) async-start(), calls=%async_computation.6 | async-start | bytes 16777216 | tf_op jit(solution)/shard_map/psum | solution.py:197
  18.1 3.8 copy-start.9
  18.1 3.8 copy-start.26
  29.4 3.8 copy-start.11
  29.4 3.8 copy-start.22
  43.2 3.8 copy-start.11
  43.2 3.8 copy-start.22
  57.0 3.8 copy-start.11
  57.0 3.8 copy-start.22
  70.8 3.8 copy-start.11
  70.8 3.8 copy-start.22
  82.8 1.1 copy-start.16
  83.8 6.0 copy-start.30
  83.8 6.0 copy-start.31
  83.8 6.0 copy-start.32
  83.8 6.1 copy-start.33
  89.5 1211.8 %all-reduce.7.cloned.1.call-start = ((), (), s32[]{:S(2)}) async-start(), calls=%async_computation.7 | async-start | bytes 16777216 | tf_op jit(solution)/shard_map/psum | solution.py:221
  383.2 7.0 copy-start.8
  383.2 8.2 copy-start.10
  394.7 12.0 copy-start.5
  394.8 7.4 copy-start.37
  402.1 4.6 copy-start.39
  406.8 3.2 copy-start.13
  406.8 206.0 %copy-start.34 = (bf16[1024]{0:T(1024)(128)(2,1)S(1)}, bf16[1024]{0:T(1024)(128)(2,1)}, u32[]{:S(2)}) copy-start(bf16[1024]{0:T(1024)(128)(2,1)} %param.38) | copy-start | bytes 6148
  406.8 206.0 %copy-start.35 = (bf16[1024]{0:T(1024)(128)(2,1)S(1)}, bf16[1024]{0:T(1024)(128)(2,1)}, u32[]{:S(2)}) copy-start(bf16[1024]{0:T(1024)(128)(2,1)} %param.37) | copy-start | bytes 6148
  406.8 206.0 %copy-start.36 = (bf16[1024]{0:T(1024)(128)(2,1)S(1)}, bf16[1024]{0:T(1024)(128)(2,1)}, u32[]{:S(2)}) copy-start(bf16[1024]{0:T(1024)(128)(2,1)} %param.39) | copy-start | bytes 6148
  406.8 182.2 %collective-permute-start = (f32[2048,1024]{1,0:T(8,128)S(1)}, f32[2048,1024]{1,0:T(8,128)}, u32[]{:S(2)}, u32[]{:S(2)}) collective-permute-start(f32[2048,1024]{1,0:T(8,128)S(1)} %fusion.71), channel_id=1, source_target_pairs={{0,1},{1,0},{2,3},{3,2},{4,5},{5,4},{6,7},{7,6},{8,9},{9,8},{10,11... | collective-permute-start | bytes 25165832 | tf_op jit(solution)/shard_map/ppermute | solution.py:19
  601.0 362.2 %collective-permute-start.1 = (f32[2048,1024]{1,0:T(8,128)}, f32[2048,1024]{1,0:T(8,128)}, u32[]{:S(2)}, u32[]{:S(2)}) collective-permute-start(f32[2048,1024]{1,0:T(8,128)} %add.205), channel_id=1, source_target_pairs={{0,2},{1,3},{2,0},{3,1},{4,6},{5,7},{6,4},{7,5},{8,10},{9,11},{10,... | collective-permute-start | bytes 25165832 | tf_op jit(solution)/shard_map/ppermute | solution.py:19
  612.9 360.7 %copy-start.28 = (pred[2048]{0:T(1024)(128)(4,1)}, pred[2048]{0:T(1024)(128)(4,1)S(1)}, u32[]{:S(2)}) copy-start(pred[2048]{0:T(1024)(128)(4,1)S(1)} %iota_compare_fusion.2) | copy-start | bytes 6148
  984.5 3.5 copy-start.6
  984.5 6.1 copy-start.7
  984.5 6.1 copy-start.38
  990.6 11.4 copy-start.14
  1001.9 2.0 copy-start.40
  1010.8 550.6 %reduce-scatter.17.cloned.1.call-start = ((), (), s32[]{:S(2)}) async-start(), calls=%async_computation.11 | async-start | bytes 2359296 | tf_op jit(solution)/shard_map/reduce_scatter | solution.py:265
  1020.5 542.7 %reduce-scatter.15.cloned.1.call-start = ((), (), s32[]{:S(2)}) async-start(), calls=%async_computation.10 | async-start | bytes 2359296 | tf_op jit(solution)/shard_map/reduce_scatter | solution.py:262
  1031.0 579.8 %reduce-scatter.19.cloned.1.call-start = ((), (), s32[]{:S(2)}) async-start(), calls=%async_computation.12 | async-start | bytes 589824
  1317.7 11.8 copy-start.24
  1327.5 2.0 copy-start.15
  1341.6 1.0 copy-start.3
  1373.2 7.2 copy-start.2
  1380.4 2.9 copy-start.4
  1383.3 1.0 copy-start.3
  1414.7 7.1 copy-start.2
  1421.9 2.9 copy-start.4
  1424.8 1.0 copy-start.3
  1456.2 7.2 copy-start.2
  1463.3 2.9 copy-start.4
  1466.2 1.0 copy-start.3
  1497.6 7.2 copy-start.2
  1504.8 2.9 copy-start.4
  1515.9 96.7 %reduce-scatter.21.cloned.1.call-start = ((), (), s32[]{:S(2)}) async-start(), calls=%async_computation.13 | async-start | bytes 589824
  1522.4 100.7 %reduce-scatter.23.cloned.1.call-start = ((), (), s32[]{:S(2)}) async-start(), calls=%async_computation.14 | async-start | bytes 589824
  1526.8 6.8 copy-start.17
  1527.9 10.2 copy-start.19
  1533.5 4.6 copy-start.25
  1533.6 126.8 %reduce-scatter.13.cloned.1.call-start = ((), (), s32[]{:S(2)}) async-start(), calls=%async_computation.9 | async-start | bytes 589824 | tf_op jit(solution)/shard_map/reduce_scatter | solution.py:259
  1538.1 4.6 copy-start.21
  1538.1 4.6 copy-start.27
  1542.6 10.1 copy-start.29
  1542.7 275.1 %all-reduce.9.cloned.1.call-start = ((), (), s32[]{:S(2)}) async-start(), calls=%async_computation.8 | async-start | bytes 8388608 | tf_op jit(solution)/shard_map/psum | solution.py:238
  1551.8 13.2 copy-start.12
  1556.8 264.5 %copy-start.1 = (bf16[1024,1024]{1,0:T(8,128)(2,1)S(1)}, bf16[1024,1024]{1,0:T(8,128)(2,1)}, u32[]{:S(2)}) copy-start(bf16[1024,1024]{1,0:T(8,128)(2,1)} %param.34) | copy-start | bytes 6291460
  (6 other events, 5.8 us)
Sparse Core Ops, SparseCore 0:
  89.6 293.5 all-reduce.4
  1010.9 290.3 all-reduce.6
  1304.6 40.0 reduce-scatter.16
  1347.9 41.1 reduce-scatter.14
  1516.0 32.6 reduce-scatter.18
  1551.6 34.2 reduce-scatter.20
  1588.9 34.1 reduce-scatter.22
  1626.2 34.1 reduce-scatter.12
  1662.7 154.9 all-reduce.8
